TPU v7x, 128 devices: a whole 4x4x4 slice. The times are simulated.
128 devices in a mesh: row: 8 (over x, y_lo), col: 8 (over z, y_hi), depth: 2 (over core).
Axes of the slice: x: 4, y: 4 (y_hi: 2, y_lo: 2; y = y_hi * 2 + y_lo), z: 4, core: 2. Of those that a mesh axis runs over, the one named last changes fastest.
Arguments:
- amplitudes: bfloat16 [20480, 20480], P('row', 'col'), may hold values from -0.109375 to 0.109375
- coulomb_vertex: bfloat16 [256, 20480], P('depth', ('row', 'col')), may hold values from -1.5 to 1.5
Outputs:
- cycle_residual: bfloat16 [20480, 20480], P('row', ('col', 'depth'))
- structure_factor: float32 [256], P('depth')
All inputs are finite; a program needn't handle non-finite values.
Results may differ from a plain program's by a relative error of at most 0.0057.
Values may be sent and summed in bfloat16 or wider, within the bound.
No kernel may reach another device: no remote copies, remote signals or barrier semaphores. Data moves between devices by JAX's collectives and lax.ppermute only.
A program may use at most 128 MiB of HBM per device.

v0:
```python
import jax
import jax.numpy as jnp
from jax import lax
from jax.sharding import PartitionSpec as P


def broadcast(array, axis, root):
    mine = lax.axis_index(axis) == root
    return lax.psum(jnp.where(mine, array, jnp.zeros_like(array)), axis)


def body(amplitudes, coulomb_vertex):
    row_index = lax.axis_index("row")
    col_index = lax.axis_index("col")
    block_width = amplitudes.shape[0]
    on_diagonal = (row_index == col_index).astype(jnp.float32)
    vertex_rows = lax.all_gather(coulomb_vertex, "col", axis=1, tiled=True)
    vertex_cols = broadcast(vertex_rows, "row", col_index)
    dressing = jnp.dot(vertex_rows, amplitudes, preferred_element_type=jnp.float32)
    factor_part = jnp.sum(dressing * vertex_cols.astype(jnp.float32), axis=1)
    structure_factor = lax.psum(factor_part, ("row", "col"))
    dressed_term = dressing + on_diagonal * vertex_rows.astype(jnp.float32)
    dressed_part = lax.psum_scatter(dressed_term, "row", scatter_dimension=1, tiled=True)
    dressed = dressed_part.astype(jnp.bfloat16)
    everything = lax.all_gather(dressed, ("row", "col"), axis=1, tiled=True)
    fields_here = everything.shape[0]
    grid_side = lax.axis_size("row")
    ordered = everything.reshape(fields_here, grid_side, grid_side, dressed.shape[1])
    ordered = jnp.transpose(ordered, (0, 2, 1, 3)).reshape(
        fields_here, grid_side * grid_side * dressed.shape[1]
    )
    dressed_cols = lax.dynamic_slice_in_dim(ordered, col_index * block_width, block_width, 1)
    dressed_rows = lax.dynamic_slice_in_dim(ordered, row_index * block_width, block_width, 1)
    cols_all = lax.all_to_all(dressed_cols, "depth", split_axis=1, concat_axis=0, tiled=True)
    rows_all = lax.all_gather(dressed_rows, "depth", axis=0, tiled=True)
    product = lax.dot_general(
        rows_all, cols_all, (((0,), (0,)), ((), ())), preferred_element_type=jnp.float32
    )
    cycle_residual = product.astype(jnp.bfloat16)
    return (cycle_residual, structure_factor)


def solution(mesh):
    return jax.shard_map(
        body,
        mesh=mesh,
        in_specs=(P("row", "col"), P("depth", ("row", "col"))),
        out_specs=(P("row", ("col", "depth")), P("depth")),
        check_vma=False,
    )
```

profile of v0, /device:TPU:1, one launch (start us, length us, event | category | flops | bytes accessed | tf_op | source)
XLA Modules:
  0.0 711.8 jit_solution(17845553352122211983)
XLA Ops:
  7.2 0.0 all-reduce.2.cloned.1.call-start
  7.2 33.1 %all_gather.9 = bf16[128,2560]{0,1:T(8,128)(2,1)S(1)} all-gather(bf16[128,320]{0,1:T(8,128)(2,1)} %param.3), channel_id=1, replica_groups=mesh['row'=8,'col'=8,'depth'=2] {'col'}, dimensions={1}, use_global_device_ids=true | all-gather | bytes 737280 | tf_op jit(solution)/shard_map/all_gather | solution.py:17
  40.3 0.2 copy.17
  40.6 0.9 broadcast_select_fusion
  41.5 0.0 all-reduce.2.cloned.1.call-update
  41.5 0.0 reduce-scatter.4.cloned.1.call-start
  41.5 77.2 %all-reduce.2.cloned.1.call-done = bf16[128,2560]{1,0:T(8,128)(2,1)} async-done(((bf16[128,2560]{1,0:T(8,128)(2,1)}), bf16[128,2560]{1,0:T(8,128)(2,1)}) %all-reduce.2.cloned.1.call-update) | async-done | bytes 655376 | tf_op jit(solution)/shard_map/psum | solution.py:9
  118.7 6.9 multiply_reduce_fusion
  125.6 1.5 copy.22
  127.1 0.0 reduce-scatter.4.cloned.1.call-update
  127.1 0.0 all-gather.3.cloned.1.call-start
  127.1 42.3 %reduce-scatter.4.cloned.1.call-done = f32[320,128]{1,0:T(8,128)} async-done(((f32[2560,128]{1,0:T(8,128)}), f32[320,128]{1,0:T(8,128)}) %reduce-scatter.4.cloned.1.call-update) | async-done | bytes 163856
  169.5 1.6 bitcast_convert_fusion
  171.0 0.0 all-gather.3.cloned.1.call-update
  171.1 0.0 all-gather.5.cloned.1.call-start
  171.1 301.0 %all-gather.3.cloned.1.call-done = bf16[128,20480]{0,1:T(8,128)(2,1)} async-done(((bf16[128,320]{0,1:T(8,128)(2,1)}), bf16[128,20480]{0,1:T(8,128)(2,1)}) %all-gather.3.cloned.1.call-update) | async-done | bytes 5242896 | tf_op jit(solution)/shard_map/all_gather | solution.py:25
  472.2 2.9 copy.19
  475.1 0.9 constant_dynamic-slice_fusion
  476.0 0.0 all-gather.5.cloned.1.call-update
  476.1 148.3 %psum.15 = f32[128]{0:T(128)} all-reduce(f32[128]{0:T(128)S(1)} %get-tuple-element.4), channel_id=1, replica_groups=mesh['row'=8,'col'=8,'depth'=2] {'row','col'}, use_global_device_ids=true, to_apply=%region_3.4 | all-reduce | flops 128 | bytes 1024 | tf_op jit(solution)/shard_map/psum | solution.py:21
  624.3 74.7 %all_to_all.19 = bf16[128,2,1280]{0,2,1:T(8,128)(2,1)S(1)} all-to-all(bf16[128,2,1280]{0,2,1:T(8,128)(2,1)S(1)} %bitcast.19), channel_id=1, replica_groups=mesh['row'=8,'col'=8,'depth'=2] {'depth'}, dimensions={1} | all-to-all | bytes 1310720 | tf_op jit(solution)/shard_map/all_to_all | solution.py:34
  699.0 0.2 copy.20
  699.3 0.0 all-gather.5.cloned.1.call-done
  699.3 6.0 convolution_convert_fusion
Async XLA Ops:
  7.2 111.5 %all-reduce.2.cloned.1.call-start = ((), (), s32[]{:S(2)}) async-start(), calls=%async_computation.4 | async-start | bytes 1310720 | tf_op jit(solution)/shard_map/psum | solution.py:9
  41.5 128.0 %reduce-scatter.4.cloned.1.call-start = ((), (), s32[]{:S(2)}) async-start(), calls=%async_computation.5 | async-start | bytes 1474560
  127.1 345.1 %all-gather.3.cloned.1.call-start = ((), (), s32[]{:S(2)}) async-start(), calls=%async_computation.2 | async-start | bytes 5324800 | tf_op jit(solution)/shard_map/all_gather | solution.py:25
  171.1 528.3 %all-gather.5.cloned.1.call-start = ((), (), s32[]{:S(2)}) async-start(), calls=%async_computation.3 | async-start | bytes 1966080 | tf_op jit(solution)/shard_map/all_gather | solution.py:35
Sparse Core Ops, SparseCore 0:
  41.6 77.0 all-reduce.1
  127.2 42.2 reduce-scatter.3
  171.7 300.4 all-gather.2
  476.2 51.9 all-gather.4
where the time goes:
time: 712 us
  waiting for transfers between devices  421 us (59%)
  blocking collectives  256 us (36%)
  between operations  13.8 us (2%)
  matrix products  12.9 us (2%)
    all_gather x1, waiting for transfers between devices, body(): everything = lax.all_gather(dressed, ('row', 'col'), axis=1, tiled=True)  301 us
    psum x1, blocking collectives, body(): structure_factor = lax.psum(factor_part, ('row', 'col'))  148 us
    psum x1, waiting for transfers between devices, broadcast(): return lax.psum(jnp.where(mine, array, jnp.zeros_like(array)), axis)  77.2 us
    all_to_all x1, blocking collectives, body(): lax.all_to_all(dressed_cols, 'depth', split_axis=1, concat_axis=0, tiled=...  74.7 us
    unnamed x5, waiting for transfers between devices  42.4 us
    all_gather x1, blocking collectives, body(): vertex_rows = lax.all_gather(coulomb_vertex, 'col', axis=1, tiled=True)  33.1 us
  transfers between devices with their start and end apart: 4, of which 3 were waited for; matrix products, arithmetic and copies ran while one was open for 0% of the time, Pallas kernels for 0%

commit v1 on v0

--- a/solution.py
+++ b/solution.py
@@ -14,7 +14,8 @@
     col_index = lax.axis_index("col")
     block_width = amplitudes.shape[0]
     on_diagonal = (row_index == col_index).astype(jnp.float32)
-    vertex_rows = lax.all_gather(coulomb_vertex, "col", axis=1, tiled=True)
+    stack = jnp.stack([coulomb_vertex] * lax.axis_size("col"))
+    vertex_rows = jnp.concatenate(lax.all_to_all(stack, "col", 0, 0), axis=1)
     vertex_cols = broadcast(vertex_rows, "row", col_index)
     dressing = jnp.dot(vertex_rows, amplitudes, preferred_element_type=jnp.float32)
     factor_part = jnp.sum(dressing * vertex_cols.astype(jnp.float32), axis=1)

time: 712 us -> 693 us (0.973)
  blocking collectives: 256 us -> 223 us
  starting transfers between devices: 0.16 us -> 8.66 us
    all_gather x1 -> x0, blocking collectives: 33.1 us -> none  [body(): vertex_rows = lax.all_gather(coulomb_vertex, 'col', axis=1, tiled=True)]
    all_to_all x0 -> x1, waiting for transfers between devices: none -> 11.7 us  [body(): vertex_rows = jnp.concatenate(lax.all_to_all(stack, 'col', 0, 0), axis=1)]
    all_to_all x0 -> x1, starting transfers between devices: none -> 8.49 us  [body(): vertex_rows = jnp.concatenate(lax.all_to_all(stack, 'col', 0, 0), axis=1)]
    psum x1, waiting for transfers between devices: 77.2 us -> 68.8 us  [broadcast(): return lax.psum(jnp.where(mine, array, jnp.zeros_like(array)), axis)]
  transfers between devices with their start and end apart: 4 -> 5, of which waited for: 3 -> 4; matrix products, arithmetic and copies ran while one was open for 0% -> 0% of each run, Pallas kernels for 0% -> 0%
where the time goes in v1:
time: 693 us; the launch traced here: 692 us
  waiting for transfers between devices  424 us (61%)
  blocking collectives  223 us (32%)
  between operations  13.8 us (2%)
  matrix products  12.9 us (2%)
  starting transfers between devices  8.66 us (1%)
  local copies, waits for them, and re-layouts  7.63 us (1%)
    all_gather x1, waiting for transfers between devices, body(): everything = lax.all_gather(dressed, ('row', 'col'), axis=1, tiled=True)  301 us
    psum x1, blocking collectives, body(): structure_factor = lax.psum(factor_part, ('row', 'col'))  148 us
    all_to_all x1, blocking collectives, body(): lax.all_to_all(dressed_cols, 'depth', split_axis=1, concat_axis=0, tiled=...  74.7 us
    psum x1, waiting for transfers between devices, broadcast(): return lax.psum(jnp.where(mine, array, jnp.zeros_like(array)), axis)  68.8 us
    unnamed x5, waiting for transfers between devices  42.3 us
  transfers between devices with their start and end apart: 5, of which 4 were waited for; matrix products, arithmetic and copies ran while one was open for 0% of the time, Pallas kernels for 0%

profile of v1, /device:TPU:1, one launch (start us, length us, event | category | flops | bytes accessed | tf_op | source)
XLA Modules:
  0.0 692.2 jit_solution(9735793142225674518)
XLA Ops:
  7.2 1.8 stack.2
  9.0 8.5 %all-to-all-start = ((bf16[8,128,320]{1,2,0:T(8,128)(2,1)}), bf16[8,128,320]{1,2,0:T(8,128)(2,1)S(1)}, u32[]{:S(2)}, u32[]{:S(2)}) async-start(bf16[8,128,320]{1,2,0:T(8,128)(2,1)} %stack.2), calls=%async_computation | async-start | bytes 1310720 | tf_op jit(solution)/shard_map/all_to_all | solution.py:18
  17.5 0.0 all-reduce.2.cloned.1.call-start
  17.5 11.7 %all-to-all-done = bf16[8,128,320]{1,2,0:T(8,128)(2,1)S(1)} async-done(((bf16[8,128,320]{1,2,0:T(8,128)(2,1)}), bf16[8,128,320]{1,2,0:T(8,128)(2,1)S(1)}, u32[]{:S(2)}, u32[]{:S(2)}) %all-to-all-start) | async-done | bytes 655392 | tf_op jit(solution)/shard_map/all_to_all | solution.py:18
  29.3 0.2 copy.19
  29.5 0.9 broadcast_select_fusion
  30.4 0.0 all-reduce.2.cloned.1.call-update
  30.4 0.0 reduce-scatter.4.cloned.1.call-start
  30.5 68.8 %all-reduce.2.cloned.1.call-done = bf16[128,2560]{1,0:T(8,128)(2,1)} async-done(((bf16[128,2560]{1,0:T(8,128)(2,1)}), bf16[128,2560]{1,0:T(8,128)(2,1)}) %all-reduce.2.cloned.1.call-update) | async-done | bytes 655376 | tf_op jit(solution)/shard_map/psum | solution.py:9
  99.3 6.9 multiply_reduce_fusion
  106.2 1.5 copy.24
  107.6 0.0 reduce-scatter.4.cloned.1.call-update
  107.6 0.0 all-gather.3.cloned.1.call-start
  107.7 42.3 %reduce-scatter.4.cloned.1.call-done = f32[320,128]{1,0:T(8,128)} async-done(((f32[2560,128]{1,0:T(8,128)}), f32[320,128]{1,0:T(8,128)}) %reduce-scatter.4.cloned.1.call-update) | async-done | bytes 163856
  150.0 1.6 bitcast_convert_fusion
  151.5 0.0 all-gather.3.cloned.1.call-update
  151.5 0.0 all-gather.5.cloned.1.call-start
  151.6 300.9 %all-gather.3.cloned.1.call-done = bf16[128,20480]{0,1:T(8,128)(2,1)} async-done(((bf16[128,320]{0,1:T(8,128)(2,1)}), bf16[128,20480]{0,1:T(8,128)(2,1)}) %all-gather.3.cloned.1.call-update) | async-done | bytes 5242896 | tf_op jit(solution)/shard_map/all_gather | solution.py:26
  452.5 2.9 copy.21
  455.5 0.9 constant_dynamic-slice_fusion
  456.4 0.0 all-gather.5.cloned.1.call-update
  456.4 148.3 %psum.15 = f32[128]{0:T(128)} all-reduce(f32[128]{0:T(128)S(1)} %get-tuple-element.4), channel_id=1, replica_groups=mesh['row'=8,'col'=8,'depth'=2] {'row','col'}, use_global_device_ids=true, to_apply=%region_3.4 | all-reduce | flops 128 | bytes 1024 | tf_op jit(solution)/shard_map/psum | solution.py:22
  604.7 74.7 %all_to_all.24 = bf16[128,2,1280]{0,2,1:T(8,128)(2,1)S(1)} all-to-all(bf16[128,2,1280]{0,2,1:T(8,128)(2,1)S(1)} %bitcast.24), channel_id=1, replica_groups=mesh['row'=8,'col'=8,'depth'=2] {'depth'}, dimensions={1} | all-to-all | bytes 1310720 | tf_op jit(solution)/shard_map/all_to_all | solution.py:35
  679.4 0.2 copy.22
  679.7 0.0 all-gather.5.cloned.1.call-done
  679.7 6.0 convolution_convert_fusion
Async XLA Ops:
  9.0 20.3 %all-to-all-start = ((bf16[8,128,320]{1,2,0:T(8,128)(2,1)}), bf16[8,128,320]{1,2,0:T(8,128)(2,1)S(1)}, u32[]{:S(2)}, u32[]{:S(2)}) async-start(bf16[8,128,320]{1,2,0:T(8,128)(2,1)} %stack.2), calls=%async_computation | async-start | bytes 1310720 | tf_op jit(solution)/shard_map/all_to_all | solution.py:18
  17.5 81.8 %all-reduce.2.cloned.1.call-start = ((), (), s32[]{:S(2)}) async-start(), calls=%async_computation.5 | async-start | bytes 1310720 | tf_op jit(solution)/shard_map/psum | solution.py:9
  30.4 119.5 %reduce-scatter.4.cloned.1.call-start = ((), (), s32[]{:S(2)}) async-start(), calls=%async_computation.6 | async-start | bytes 1474560
  107.6 344.9 %all-gather.3.cloned.1.call-start = ((), (), s32[]{:S(2)}) async-start(), calls=%async_computation.3 | async-start | bytes 5324800 | tf_op jit(solution)/shard_map/all_gather | solution.py:26
  151.5 528.2 %all-gather.5.cloned.1.call-start = ((), (), s32[]{:S(2)}) async-start(), calls=%async_computation.4 | async-start | bytes 1966080 | tf_op jit(solution)/shard_map/all_gather | solution.py:36
Sparse Core Ops, SparseCore 0:
  30.5 68.6 all-reduce.1
  107.8 42.1 reduce-scatter.3
  152.2 300.3 all-gather.2
  456.5 51.9 all-gather.4

commit v2 on v0

--- a/solution.py
+++ b/solution.py
@@ -18,7 +18,8 @@
     vertex_cols = broadcast(vertex_rows, "row", col_index)
     dressing = jnp.dot(vertex_rows, amplitudes, preferred_element_type=jnp.float32)
     factor_part = jnp.sum(dressing * vertex_cols.astype(jnp.float32), axis=1)
-    structure_factor = lax.psum(factor_part, ("row", "col"))
+    half = lax.psum(factor_part, "row")
+    structure_factor = lax.psum(half, "col")
     dressed_term = dressing + on_diagonal * vertex_rows.astype(jnp.float32)
     dressed_part = lax.psum_scatter(dressed_term, "row", scatter_dimension=1, tiled=True)
     dressed = dressed_part.astype(jnp.bfloat16)

time: 712 us -> 577 us (0.81)
  blocking collectives: 256 us -> 121 us
    psum x1 -> x2, blocking collectives: 148 us -> 33.4 us  [the longest x1 19.8 us: body(): structure_factor = lax.psum(half, 'col')]
    all_to_all x1, blocking collectives: 74.7 us -> 54.2 us  [body(): lax.all_to_all(dressed_cols, 'depth', split_axis=1, concat_axis=0, tiled=...]
where the time goes in v2:
time: 577 us
  waiting for transfers between devices  421 us (73%)
  blocking collectives  121 us (21%)
  between operations  13.8 us (2%)
  matrix products  12.9 us (2%)
  local copies, waits for them, and re-layouts  5.82 us (1%)
    all_gather x1, waiting for transfers between devices, body(): everything = lax.all_gather(dressed, ('row', 'col'), axis=1, tiled=True)  301 us
    psum x1, waiting for transfers between devices, broadcast(): return lax.psum(jnp.where(mine, array, jnp.zeros_like(array)), axis)  77.2 us
    all_to_all x1, blocking collectives, body(): lax.all_to_all(dressed_cols, 'depth', split_axis=1, concat_axis=0, tiled=...  54.2 us
    unnamed x5, waiting for transfers between devices  42.4 us
    all_gather x1, blocking collectives, body(): vertex_rows = lax.all_gather(coulomb_vertex, 'col', axis=1, tiled=True)  33.1 us
    psum x1, blocking collectives, body(): structure_factor = lax.psum(half, 'col')  19.8 us
    psum x1, blocking collectives, body(): half = lax.psum(factor_part, 'row')  13.7 us
  transfers between devices with their start and end apart: 4, of which 3 were waited for; matrix products, arithmetic and copies ran while one was open for 0% of the time, Pallas kernels for 0%

profile of v2, /device:TPU:1, one launch (start us, length us, event | category | flops | bytes accessed | tf_op | source)
XLA Modules:
  0.0 576.5 jit_solution(13179857993816247356)
XLA Ops:
  7.2 0.0 all-reduce.2.cloned.1.call-start
  7.2 33.1 %all_gather.9 = bf16[128,2560]{0,1:T(8,128)(2,1)S(1)} all-gather(bf16[128,320]{0,1:T(8,128)(2,1)} %param.3), channel_id=1, replica_groups=mesh['row'=8,'col'=8,'depth'=2] {'col'}, dimensions={1}, use_global_device_ids=true | all-gather | bytes 737280 | tf_op jit(solution)/shard_map/all_gather | solution.py:17
  40.3 0.2 copy.17
  40.6 0.9 broadcast_select_fusion
  41.5 0.0 all-reduce.2.cloned.1.call-update
  41.5 0.0 reduce-scatter.4.cloned.1.call-start
  41.5 77.2 %all-reduce.2.cloned.1.call-done = bf16[128,2560]{1,0:T(8,128)(2,1)} async-done(((bf16[128,2560]{1,0:T(8,128)(2,1)}), bf16[128,2560]{1,0:T(8,128)(2,1)}) %all-reduce.2.cloned.1.call-update) | async-done | bytes 655376 | tf_op jit(solution)/shard_map/psum | solution.py:9
  118.7 6.9 %multiply_reduce_fusion = (f32[128]{0:T(128)S(1)}, f32[128,2560]{1,0:T(8,128)S(1)}) fusion(bf16[128,2560]{1,0:T(8,128)(2,1)} %all-reduce.2.cloned.1.call-done, bf16[128,2560]{1,0:T(8,128)(2,1)S(1)} %copy.17, f32[]{:T(128)S(6)} %convert_element_type.15, bf16[128,2560]{0,1:T(8,128)(2,1)S(1)} %all_gather.9, bf16[2560,2560]{1,0:T(8,128)(2,1)} %param.2), kind=kOutput, calls=%fused_computation.1 | convolution fusion | flops 1679687552 | bytes 16384516 | tf_op jit(solution)/shard_map/dot_general | solution.py:19
  125.6 1.5 copy.22
  127.1 0.0 reduce-scatter.4.cloned.1.call-update
  127.1 0.0 all-gather.3.cloned.1.call-start
  127.1 42.3 %reduce-scatter.4.cloned.1.call-done = f32[320,128]{1,0:T(8,128)} async-done(((f32[2560,128]{1,0:T(8,128)}), f32[320,128]{1,0:T(8,128)}) %reduce-scatter.4.cloned.1.call-update) | async-done | bytes 163856
  169.5 1.6 bitcast_convert_fusion
  171.0 0.0 all-gather.3.cloned.1.call-update
  171.1 0.0 all-gather.5.cloned.1.call-start
  171.1 301.0 %all-gather.3.cloned.1.call-done = bf16[128,20480]{0,1:T(8,128)(2,1)} async-done(((bf16[128,320]{0,1:T(8,128)(2,1)}), bf16[128,20480]{0,1:T(8,128)(2,1)}) %all-gather.3.cloned.1.call-update) | async-done | bytes 5242896 | tf_op jit(solution)/shard_map/all_gather | solution.py:26
  472.2 2.9 copy.19
  475.1 0.9 constant_dynamic-slice_fusion
  476.0 0.0 all-gather.5.cloned.1.call-update
  476.1 13.7 %psum.22 = f32[128]{0:T(128)S(1)} all-reduce(f32[128]{0:T(128)S(1)} %get-tuple-element.4), channel_id=1, replica_groups=mesh['row'=8,'col'=8,'depth'=2] {'row'}, use_global_device_ids=true, to_apply=%region_3.4 | all-reduce | flops 128 | bytes 1024 | tf_op jit(solution)/shard_map/psum | solution.py:21
  489.7 19.8 %psum.23 = f32[128]{0:T(128)} all-reduce(f32[128]{0:T(128)S(1)} %psum.22), channel_id=1, replica_groups=mesh['row'=8,'col'=8,'depth'=2] {'col'}, use_global_device_ids=true, to_apply=%region_4.5 | all-reduce | flops 128 | bytes 1024 | tf_op jit(solution)/shard_map/psum | solution.py:22
  509.5 54.2 %all_to_all.19 = bf16[128,2,1280]{0,2,1:T(8,128)(2,1)S(1)} all-to-all(bf16[128,2,1280]{0,2,1:T(8,128)(2,1)S(1)} %bitcast.19), channel_id=1, replica_groups=mesh['row'=8,'col'=8,'depth'=2] {'depth'}, dimensions={1} | all-to-all | bytes 1310720 | tf_op jit(solution)/shard_map/all_to_all | solution.py:35
  563.7 0.2 copy.20
  564.0 0.0 all-gather.5.cloned.1.call-done
  564.0 6.0 %convolution_convert_fusion = bf16[2560,1280]{1,0:T(8,128)(2,1)} fusion(bf16[256,2560]{0,1:T(8,128)(2,1)} %all-gather.5.cloned.1.call-done, bf16[256,1280]{1,0:T(8,128)(2,1)S(1)} %bitcast.17), kind=kOutput, calls=%fused_computation | convolution fusion | flops 1680998400 | bytes 8519680 | tf_op jit(solution)/shard_map/dot_general | solution.py:37
Async XLA Ops:
  7.2 111.5 %all-reduce.2.cloned.1.call-start = ((), (), s32[]{:S(2)}) async-start(), calls=%async_computation.4 | async-start | bytes 1310720 | tf_op jit(solution)/shard_map/psum | solution.py:9
  41.5 128.0 %reduce-scatter.4.cloned.1.call-start = ((), (), s32[]{:S(2)}) async-start(), calls=%async_computation.5 | async-start | bytes 1474560
  127.1 345.1 %all-gather.3.cloned.1.call-start = ((), (), s32[]{:S(2)}) async-start(), calls=%async_computation.2 | async-start | bytes 5324800 | tf_op jit(solution)/shard_map/all_gather | solution.py:26
  171.1 393.0 %all-gather.5.cloned.1.call-start = ((), (), s32[]{:S(2)}) async-start(), calls=%async_computation.3 | async-start | bytes 1966080 | tf_op jit(solution)/shard_map/all_gather | solution.py:36
Sparse Core Ops, SparseCore 0:
  41.6 77.0 all-reduce.1
  127.2 42.2 reduce-scatter.3
  171.7 300.4 all-gather.2
  476.2 51.8 all-gather.4
